TPU v7x, 32 devices: a whole 2x2x4 slice. The times are simulated.
32 devices in a mesh: row: 2 (over x), col: 16 (over z, y, core).
Axes of the slice: x: 2, y: 2, z: 4, core: 2. Of those that a mesh axis runs over, the one named last changes fastest.
Arguments:
- features: bfloat16 [8192, 256], P(('row', 'col')), may hold values from -6 to 6
- weight: bfloat16 [256, 128], replicated, may hold values from -0.375 to 0.375
- tiles: bfloat16 [2, 16, 320, 128, 128], P('row', 'col'), may hold values from -0.0625 to 0.0625
- slot_tile_row: int32 [2, 16, 320], P('row', 'col'), may hold values from 0 to 3
- tile_cols: int32 [2, 16, 320], P('row', 'col'), may hold values from 0 to 31
- live_tiles: int32 [2, 16], P('row', 'col'), may hold values from 40 to 320, as said below
- cotangent: bfloat16 [8192, 128], P(('row', 'col')), may hold values from -6 to 6
Outputs:
- logits: bfloat16 [8192, 128], P(('row', 'col'))
- grad_features: bfloat16 [8192, 256], P(('row', 'col'))
- grad_weight: float32 [256, 128], replicated
Inputs may be any that keep to these rules, and one draw needn't show every extreme that they name: Slots of a block from live_tiles on are padding and not part of the adjacency; in every draw some block has all 320 slots live.
All inputs are finite; a program needn't handle non-finite values.
Results may differ from a plain program's by a relative error of at most 0.005.
Values may be sent and summed in bfloat16 or wider, within the bound.
A program may use at most 128 MiB of HBM per device.

v0:
```python
import math
import jax
import jax.numpy as jnp
from jax import lax
from jax.sharding import PartitionSpec as P


def per_device(features, weight, tiles, slot_tile_row, tile_cols, live_tiles, cotangent):
    tile_block = tiles[0, 0]
    slot_rows = slot_tile_row[0, 0]
    slot_cols = tile_cols[0, 0]
    live_count = live_tiles[0, 0]
    tile_extent = tile_block.shape[-1]
    slot_total = tile_block.shape[0]
    stretch_rows = features.shape[0]
    output_width = weight.shape[1]
    row_count = lax.axis_size("row")
    col_count = lax.axis_size("col")
    row_tiles = row_count * stretch_rows // tile_extent
    col_tiles = col_count * stretch_rows // tile_extent
    block_size = 64
    block_total = slot_total // block_size
    projected_group = jnp.dot(
        lax.all_gather(features, "col", axis=0, tiled=True),
        weight,
        preferred_element_type=jnp.float32,
    ).astype(jnp.bfloat16)
    proj_tiles = projected_group.reshape(col_tiles, tile_extent, output_width)

    def block_slice(first_slot):
        part_tiles = lax.dynamic_slice_in_dim(tile_block, first_slot, block_size, 0)
        part_rows = lax.dynamic_slice_in_dim(slot_rows, first_slot, block_size, 0)
        part_cols = lax.dynamic_slice_in_dim(slot_cols, first_slot, block_size, 0)
        live_mask = first_slot + jnp.arange(block_size, dtype=jnp.int32) < live_count
        return (part_tiles, part_rows, part_cols, live_mask)

    def forward_block(block_index, totals):
        part_tiles, part_rows, part_cols, live_mask = block_slice(block_index * block_size)
        inputs = proj_tiles[part_cols]
        products = jnp.einsum(
            "tab,tbf->taf", part_tiles, inputs, preferred_element_type=jnp.float32
        )
        segment_ids = jnp.where(live_mask, part_rows, row_tiles)
        summed = jax.ops.segment_sum(products, segment_ids, num_segments=row_tiles + 1)
        return totals + summed[:row_tiles]

    forward_totals = lax.fori_loop(
        0,
        block_total,
        forward_block,
        jnp.zeros((row_tiles, tile_extent, output_width), jnp.float32),
    )
    logits = lax.psum_scatter(
        forward_totals.reshape(row_tiles * tile_extent, output_width),
        "row",
        scatter_dimension=0,
        tiled=True,
    ).astype(jnp.bfloat16)
    cot_group = lax.all_gather(cotangent, "row", axis=0, tiled=True)
    cot_tiles = cot_group.reshape(row_tiles, tile_extent, output_width)

    def backward_block(block_index, totals):
        part_tiles, part_rows, part_cols, live_mask = block_slice(block_index * block_size)
        inputs = cot_tiles[part_rows]
        products = jnp.einsum(
            "tab,taf->tbf", part_tiles, inputs, preferred_element_type=jnp.float32
        )
        inside = live_mask & (part_cols >= 0) & (part_cols < col_tiles)
        segment_ids = jnp.where(inside, part_cols, col_tiles)
        summed = jax.ops.segment_sum(products, segment_ids, num_segments=col_tiles + 1)
        return totals + summed[:col_tiles]

    empty = jnp.zeros((col_tiles, tile_extent, output_width), jnp.float32)
    backward_totals = lax.fori_loop(0, block_total, backward_block, empty).reshape(
        col_tiles * tile_extent, output_width
    )
    back = lax.psum_scatter(backward_totals, "col", scatter_dimension=0, tiled=True)
    back_rounded = back.astype(jnp.bfloat16)
    grad_features = jnp.dot(back_rounded, weight.T, preferred_element_type=jnp.float32).astype(
        jnp.bfloat16
    )
    weight_term = lax.dot_general(
        features, back_rounded, (((0,), (0,)), ((), ())), preferred_element_type=jnp.float32
    )
    node_total = stretch_rows * row_count * col_count
    grad_weight = lax.psum(weight_term, ("row", "col")) / math.sqrt(node_total)
    return (logits, grad_features, grad_weight)


def solution(mesh):
    placed = (
        P(("row", "col"), None),
        P(),
        P("row", "col", None, None, None),
        P("row", "col", None),
        P("row", "col", None),
        P("row", "col"),
        P(("row", "col"), None),
    )
    return jax.shard_map(
        per_device,
        mesh=mesh,
        in_specs=placed,
        out_specs=(P(("row", "col"), None), P(("row", "col"), None), P()),
        check_vma=False,
    )
```

profile of v0, /device:TPU:0, one launch (start us, length us, event | category | flops | bytes accessed | tf_op | source)
XLA Modules:
  0.0 375.7 jit_solution(15768739046971264460)
XLA Ops:
  8.6 14.4 %copy.10 = bf16[1,1,320,128,128]{3,4,2,1,0:T(8,128)(2,1)} copy(bf16[1,1,320,128,128]{4,3,2,1,0:T(8,128)(2,1)} %param.13) | data formatting | bytes 20971520 | tf_op args[2]
  23.0 5.9 %all_gather.7 = bf16[512,128]{1,0:T(8,128)(2,1)S(1)} all-gather(bf16[256,128]{1,0:T(8,128)(2,1)S(1)} %copy-done.3), channel_id=1, replica_groups=mesh['row'=2,'col'=16] {'row'}, dimensions={0}, use_global_device_ids=true | all-gather | bytes 196608 | tf_op jit(solution)/shard_map/all_gather | solution.py:59
  28.9 90.2 %while.29 = (s32[]{:T(128)}, f32[32,128,128]{2,1,0:T(8,128)}, s32[]{:T(128)}, s32[320]{0:T(512)S(1)}, bf16[320,128,128]{1,2,0:T(8,128)(2,1)}, /*index=5*/s32[320...) while((s32[]{:T(128)}, f32[32,128,128]{2,1,0:T(8,128)}, ...), condition=%wide.region_6.7_spmd.clone, body=%wide.region_4.6_spmd.clone.sunk | while | flops 270534272 | bytes 33626048 | solution.py:74
  29.6 1.0 gather_fusion.1
  30.6 4.4 %fusion.25 = f32[64,128,128]{2,1,0:T(8,128)} fusion(bf16[64,128,128]{2,1,0:T(8,128)(2,1)S(1)} %gather_fusion.1, bf16[320,128,128]{1,2,0:T(8,128)(2,1)} %get-tuple-element.501, s32[]{:T(128)S(6)} %select_n.64), kind=kOutput, calls=%fused_computation.12.clone.1 | convolution fusion | flops 268435456 | bytes 8388612 | tf_op jit(solution)/shard_map/while/body/eval_jaxpr/tab,taf->tbf/dot_general | solution.py:65
  35.2 8.8 %scatter_fusion.1 = f32[33,128,128]{2,1,0:T(8,128)S(1)} fusion(f32[33,128,128]{2,1,0:T(8,128)S(1)} %broadcast.112, s32[64]{0:T(128)S(1)} %get-tuple-element.435, f32[64,128,128]{2,1,0:T(8,128)} %fusion.25), kind=kCustom, calls=%fused_computation.3.clone.clone.1 | custom fusion | flops 1048576 | bytes 12583168 | tf_op jit(solution)/shard_map/while/body/eval_jaxpr/scatter-add | solution.py:70
  44.0 1.6 slice_add_fusion.5
  46.4 1.0 gather_fusion.1
  47.4 4.4 %fusion.25 = f32[64,128,128]{2,1,0:T(8,128)} fusion(bf16[64,128,128]{2,1,0:T(8,128)(2,1)S(1)} %gather_fusion.1, bf16[320,128,128]{1,2,0:T(8,128)(2,1)} %get-tuple-element.501, s32[]{:T(128)S(6)} %select_n.64), kind=kOutput, calls=%fused_computation.12.clone.1 | convolution fusion | flops 268435456 | bytes 8388612 | tf_op jit(solution)/shard_map/while/body/eval_jaxpr/tab,taf->tbf/dot_general | solution.py:65
  52.0 8.8 %scatter_fusion.1 = f32[33,128,128]{2,1,0:T(8,128)S(1)} fusion(f32[33,128,128]{2,1,0:T(8,128)S(1)} %broadcast.112, s32[64]{0:T(128)S(1)} %get-tuple-element.435, f32[64,128,128]{2,1,0:T(8,128)} %fusion.25), kind=kCustom, calls=%fused_computation.3.clone.clone.1 | custom fusion | flops 1048576 | bytes 12583168 | tf_op jit(solution)/shard_map/while/body/eval_jaxpr/scatter-add | solution.py:70
  60.8 3.2 slice_add_fusion.5
  64.8 1.0 gather_fusion.1
  65.7 4.4 %fusion.25 = f32[64,128,128]{2,1,0:T(8,128)} fusion(bf16[64,128,128]{2,1,0:T(8,128)(2,1)S(1)} %gather_fusion.1, bf16[320,128,128]{1,2,0:T(8,128)(2,1)} %get-tuple-element.501, s32[]{:T(128)S(6)} %select_n.64), kind=kOutput, calls=%fused_computation.12.clone.1 | convolution fusion | flops 268435456 | bytes 8388612 | tf_op jit(solution)/shard_map/while/body/eval_jaxpr/tab,taf->tbf/dot_general | solution.py:65
  70.3 8.8 %scatter_fusion.1 = f32[33,128,128]{2,1,0:T(8,128)S(1)} fusion(f32[33,128,128]{2,1,0:T(8,128)S(1)} %broadcast.112, s32[64]{0:T(128)S(1)} %get-tuple-element.435, f32[64,128,128]{2,1,0:T(8,128)} %fusion.25), kind=kCustom, calls=%fused_computation.3.clone.clone.1 | custom fusion | flops 1048576 | bytes 12583168 | tf_op jit(solution)/shard_map/while/body/eval_jaxpr/scatter-add | solution.py:70
  79.2 3.2 slice_add_fusion.5
  83.1 1.0 gather_fusion.1
  84.1 4.4 %fusion.25 = f32[64,128,128]{2,1,0:T(8,128)} fusion(bf16[64,128,128]{2,1,0:T(8,128)(2,1)S(1)} %gather_fusion.1, bf16[320,128,128]{1,2,0:T(8,128)(2,1)} %get-tuple-element.501, s32[]{:T(128)S(6)} %select_n.64), kind=kOutput, calls=%fused_computation.12.clone.1 | convolution fusion | flops 268435456 | bytes 8388612 | tf_op jit(solution)/shard_map/while/body/eval_jaxpr/tab,taf->tbf/dot_general | solution.py:65
  88.7 8.8 %scatter_fusion.1 = f32[33,128,128]{2,1,0:T(8,128)S(1)} fusion(f32[33,128,128]{2,1,0:T(8,128)S(1)} %broadcast.112, s32[64]{0:T(128)S(1)} %get-tuple-element.435, f32[64,128,128]{2,1,0:T(8,128)} %fusion.25), kind=kCustom, calls=%fused_computation.3.clone.clone.1 | custom fusion | flops 1048576 | bytes 12583168 | tf_op jit(solution)/shard_map/while/body/eval_jaxpr/scatter-add | solution.py:70
  97.5 3.2 slice_add_fusion.5
  101.5 1.0 gather_fusion.1
  102.4 4.4 %fusion.25 = f32[64,128,128]{2,1,0:T(8,128)} fusion(bf16[64,128,128]{2,1,0:T(8,128)(2,1)S(1)} %gather_fusion.1, bf16[320,128,128]{1,2,0:T(8,128)(2,1)} %get-tuple-element.501, s32[]{:T(128)S(6)} %select_n.64), kind=kOutput, calls=%fused_computation.12.clone.1 | convolution fusion | flops 268435456 | bytes 8388612 | tf_op jit(solution)/shard_map/while/body/eval_jaxpr/tab,taf->tbf/dot_general | solution.py:65
  107.1 8.8 %scatter_fusion.1 = f32[33,128,128]{2,1,0:T(8,128)S(1)} fusion(f32[33,128,128]{2,1,0:T(8,128)S(1)} %broadcast.112, s32[64]{0:T(128)S(1)} %get-tuple-element.435, f32[64,128,128]{2,1,0:T(8,128)} %fusion.25), kind=kCustom, calls=%fused_computation.3.clone.clone.1 | custom fusion | flops 1048576 | bytes 12583168 | tf_op jit(solution)/shard_map/while/body/eval_jaxpr/scatter-add | solution.py:70
  115.9 3.2 slice_add_fusion.5
  119.9 62.9 %reduce-scatter.5.cloned.1.call-done = f32[256,128]{1,0:T(8,128)} async-done(((f32[4096,128]{1,0:T(8,128)}), f32[256,128]{1,0:T(8,128)}) %reduce-scatter.5.cloned.1.call-update) | async-done | bytes 131088 | tf_op jit(solution)/shard_map/reduce_scatter | solution.py:77
  182.8 1.8 convolution_bitcast_fusion
  184.6 40.8 %all-gather.2.cloned.1.call-done = bf16[4096,256]{1,0:T(8,128)(2,1)} async-done(((bf16[256,256]{1,0:T(8,128)(2,1)}), bf16[4096,256]{1,0:T(8,128)(2,1)}) %all-gather.2.cloned.1.call-update) | async-done | bytes 2097168 | tf_op jit(solution)/shard_map/all_gather | solution.py:24
  225.4 2.3 convolution_convert_fusion
  227.7 74.2 %while.28 = (s32[]{:T(128)}, f32[4,128,128]{2,1,0:T(8,128)S(1)}, s32[]{:T(128)}, s32[320]{0:T(512)S(1)}, bf16[320,128,128]{2,1,0:T(8,128)(2,1)}, /*index=5*/s32[...) while((s32[]{:T(128)}, f32[4,128,128]{2,1,0:T(8,128)S(1)}, ...), condition=%wide.region_2.3_spmd.clone, body=%wide.region_0.2_spmd.clone.sunk | while | flops 269616512 | bytes 26286016 | solution.py:47
  228.4 1.0 gather_fusion
  229.4 4.2 %fusion.22 = f32[64,128,128]{2,1,0:T(8,128)} fusion(bf16[64,128,128]{2,1,0:T(8,128)(2,1)S(1)} %gather_fusion, bf16[320,128,128]{2,1,0:T(8,128)(2,1)} %get-tuple-element.465, s32[]{:T(128)S(6)} %select_n.62), kind=kOutput, calls=%fused_computation.4.clone.1 | convolution fusion | flops 268435456 | bytes 8388612 | tf_op jit(solution)/shard_map/while/body/eval_jaxpr/tab,tbf->taf/dot_general | solution.py:40
  233.7 8.8 %scatter_fusion = f32[5,128,128]{2,1,0:T(8,128)S(1)} fusion(f32[5,128,128]{2,1,0:T(8,128)S(1)} %broadcast.105, s32[64]{0:T(128)S(1)} %get-tuple-element.426, f32[64,128,128]{2,1,0:T(8,128)} %fusion.22), kind=kCustom, calls=%fused_computation.2.clone.clone.1 | custom fusion | flops 1048576 | bytes 12583168 | tf_op jit(solution)/shard_map/while/body/eval_jaxpr/scatter-add | solution.py:44
  243.3 1.0 gather_fusion
  244.2 4.2 %fusion.22 = f32[64,128,128]{2,1,0:T(8,128)} fusion(bf16[64,128,128]{2,1,0:T(8,128)(2,1)S(1)} %gather_fusion, bf16[320,128,128]{2,1,0:T(8,128)(2,1)} %get-tuple-element.465, s32[]{:T(128)S(6)} %select_n.62), kind=kOutput, calls=%fused_computation.4.clone.1 | convolution fusion | flops 268435456 | bytes 8388612 | tf_op jit(solution)/shard_map/while/body/eval_jaxpr/tab,tbf->taf/dot_general | solution.py:40
  248.5 8.8 %scatter_fusion = f32[5,128,128]{2,1,0:T(8,128)S(1)} fusion(f32[5,128,128]{2,1,0:T(8,128)S(1)} %broadcast.105, s32[64]{0:T(128)S(1)} %get-tuple-element.426, f32[64,128,128]{2,1,0:T(8,128)} %fusion.22), kind=kCustom, calls=%fused_computation.2.clone.clone.1 | custom fusion | flops 1048576 | bytes 12583168 | tf_op jit(solution)/shard_map/while/body/eval_jaxpr/scatter-add | solution.py:44
  258.1 1.0 gather_fusion
  259.1 4.2 %fusion.22 = f32[64,128,128]{2,1,0:T(8,128)} fusion(bf16[64,128,128]{2,1,0:T(8,128)(2,1)S(1)} %gather_fusion, bf16[320,128,128]{2,1,0:T(8,128)(2,1)} %get-tuple-element.465, s32[]{:T(128)S(6)} %select_n.62), kind=kOutput, calls=%fused_computation.4.clone.1 | convolution fusion | flops 268435456 | bytes 8388612 | tf_op jit(solution)/shard_map/while/body/eval_jaxpr/tab,tbf->taf/dot_general | solution.py:40
  263.4 8.8 %scatter_fusion = f32[5,128,128]{2,1,0:T(8,128)S(1)} fusion(f32[5,128,128]{2,1,0:T(8,128)S(1)} %broadcast.105, s32[64]{0:T(128)S(1)} %get-tuple-element.426, f32[64,128,128]{2,1,0:T(8,128)} %fusion.22), kind=kCustom, calls=%fused_computation.2.clone.clone.1 | custom fusion | flops 1048576 | bytes 12583168 | tf_op jit(solution)/shard_map/while/body/eval_jaxpr/scatter-add | solution.py:44
  273.0 1.0 gather_fusion
  273.9 4.2 %fusion.22 = f32[64,128,128]{2,1,0:T(8,128)} fusion(bf16[64,128,128]{2,1,0:T(8,128)(2,1)S(1)} %gather_fusion, bf16[320,128,128]{2,1,0:T(8,128)(2,1)} %get-tuple-element.465, s32[]{:T(128)S(6)} %select_n.62), kind=kOutput, calls=%fused_computation.4.clone.1 | convolution fusion | flops 268435456 | bytes 8388612 | tf_op jit(solution)/shard_map/while/body/eval_jaxpr/tab,tbf->taf/dot_general | solution.py:40
  278.2 8.8 %scatter_fusion = f32[5,128,128]{2,1,0:T(8,128)S(1)} fusion(f32[5,128,128]{2,1,0:T(8,128)S(1)} %broadcast.105, s32[64]{0:T(128)S(1)} %get-tuple-element.426, f32[64,128,128]{2,1,0:T(8,128)} %fusion.22), kind=kCustom, calls=%fused_computation.2.clone.clone.1 | custom fusion | flops 1048576 | bytes 12583168 | tf_op jit(solution)/shard_map/while/body/eval_jaxpr/scatter-add | solution.py:44
  287.8 1.0 gather_fusion
  288.8 4.2 %fusion.22 = f32[64,128,128]{2,1,0:T(8,128)} fusion(bf16[64,128,128]{2,1,0:T(8,128)(2,1)S(1)} %gather_fusion, bf16[320,128,128]{2,1,0:T(8,128)(2,1)} %get-tuple-element.465, s32[]{:T(128)S(6)} %select_n.62), kind=kOutput, calls=%fused_computation.4.clone.1 | convolution fusion | flops 268435456 | bytes 8388612 | tf_op jit(solution)/shard_map/while/body/eval_jaxpr/tab,tbf->taf/dot_general | solution.py:40
  293.1 8.8 %scatter_fusion = f32[5,128,128]{2,1,0:T(8,128)S(1)} fusion(f32[5,128,128]{2,1,0:T(8,128)S(1)} %broadcast.105, s32[64]{0:T(128)S(1)} %get-tuple-element.426, f32[64,128,128]{2,1,0:T(8,128)} %fusion.22), kind=kCustom, calls=%fused_computation.2.clone.clone.1 | custom fusion | flops 1048576 | bytes 12583168 | tf_op jit(solution)/shard_map/while/body/eval_jaxpr/scatter-add | solution.py:44
  302.7 1.8 convolution_convert_fusion.1
  304.4 50.3 %all-reduce.2.cloned.1.call-done = f32[256,128]{0,1:T(8,128)} async-done(((f32[256,128]{0,1:T(8,128)}), f32[256,128]{0,1:T(8,128)}) %all-reduce.2.cloned.1.call-update) | async-done | bytes 131088 | tf_op jit(solution)/shard_map/psum | solution.py:86
  354.7 0.9 broadcast_multiply_fusion
  356.4 11.2 %reduce-scatter.3.cloned.1.call-done = f32[256,128]{1,0:T(8,128)} async-done(((f32[512,128]{1,0:T(8,128)}), f32[256,128]{1,0:T(8,128)}) %reduce-scatter.3.cloned.1.call-update) | async-done | bytes 131088 | tf_op jit(solution)/shard_map/reduce_scatter | solution.py:53
  367.6 1.5 convert_element_type.13
  (56 shorter events, 12.8 us)
Async XLA Ops:
  7.2 218.2 %copy-start = (bf16[256,128]{1,0:T(8,128)(2,1)S(1)}, bf16[256,128]{1,0:T(8,128)(2,1)}, u32[]{:S(2)}) copy-start(bf16[256,128]{1,0:T(8,128)(2,1)} %param.12) | copy-start | bytes 196612
  7.2 175.6 %reduce-scatter.5.cloned.1.call-start = ((), (), s32[]{:S(2)}) async-start(), calls=%async_computation.4 | async-start | bytes 2228224 | tf_op jit(solution)/shard_map/reduce_scatter | solution.py:77
  8.6 14.4 %copy-start.3 = (bf16[256,128]{1,0:T(8,128)(2,1)S(1)}, bf16[256,128]{1,0:T(8,128)(2,1)}, u32[]{:S(2)}) copy-start(bf16[256,128]{1,0:T(8,128)(2,1)} %param.17) | copy-start | bytes 196612
  119.1 63.7 %copy-start.2 = (bf16[256,256]{1,0:T(8,128)(2,1)S(1)}, bf16[256,256]{1,0:T(8,128)(2,1)}, u32[]{:S(2)}) copy-start(bf16[256,256]{1,0:T(8,128)(2,1)} %param.11) | copy-start | bytes 393220
  119.1 106.3 %all-gather.2.cloned.1.call-start = ((), (), s32[]{:S(2)}) async-start(), calls=%async_computation.2 | async-start | bytes 2228224 | tf_op jit(solution)/shard_map/all_gather | solution.py:24
  119.9 234.9 %all-reduce.2.cloned.1.call-start = ((), (), s32[]{:S(2)}) async-start(), calls=%async_computation.5 | async-start | bytes 262144 | tf_op jit(solution)/shard_map/psum | solution.py:86
  184.6 183.1 %reduce-scatter.3.cloned.1.call-start = ((), (), s32[]{:S(2)}) async-start(), calls=%async_computation.3 | async-start | bytes 393216 | tf_op jit(solution)/shard_map/reduce_scatter | solution.py:53
  301.9 0.7 copy-start.1
Sparse Core Ops, SparseCore 0:
  119.3 63.4 reduce-scatter.4
  185.0 40.3 all-gather.1
  231.5 123.1 all-reduce.1
  356.8 10.7 reduce-scatter.2
where the time goes:
time: 378 us; the launch traced here: 376 us
  waiting for transfers between devices  166 us (44%)
  other arithmetic  114 us (30%)
  matrix products  48.8 us (13%)
  local copies, waits for them, and re-layouts  26.7 us (7%)
  between operations  13.8 us (4%)
  blocking collectives  5.85 us (2%)
    reduce_scatter x1, waiting for transfers between devices, per_device(): lax.psum_scatter(backward_totals, 'col', scatter_dimension=0, tiled=True)  62.9 us
    psum x1, waiting for transfers between devices, per_device(): grad_weight = lax.psum(weight_term, ('row', 'col')) / math.sqrt(node_total)  50.3 us
    scatter-add x5, other arithmetic, backward_block(): jax.ops.segment_sum(products, segment_ids, num_segments=col_tiles + 1)  44 us
    scatter-add x5, other arithmetic, forward_block(): jax.ops.segment_sum(products, segment_ids, num_segments=row_tiles + 1)  43.9 us
    all_gather x1, waiting for transfers between devices, per_device(): lax.all_gather(features, 'col', axis=0, tiled=True)  40.8 us
    dot_general x5, matrix products, backward_block(): jnp.einsum('tab,taf->tbf', part_tiles, inputs, preferred_element_type=jnp...  21.9 us
    dot_general x5, matrix products, forward_block(): jnp.einsum('tab,tbf->taf', part_tiles, inputs, preferred_element_type=jnp...  21.1 us
    unnamed x10, local copies, waits for them, and re-layouts  15.9 us
  transfers between devices with their start and end apart: 4, of which 4 were waited for; matrix products, arithmetic and copies ran while one was open for 22% of the time, Pallas kernels for 0%

commit v1 on v0

--- a/solution.py
+++ b/solution.py
@@ -83,7 +83,9 @@
         features, back_rounded, (((0,), (0,)), ((), ())), preferred_element_type=jnp.float32
     )
     node_total = stretch_rows * row_count * col_count
-    grad_weight = lax.psum(weight_term, ("row", "col")) / math.sqrt(node_total)
+    grad_weight = jnp.sum(lax.all_gather(weight_term, ("row", "col")), axis=0) / math.sqrt(
+        node_total
+    )
     return (logits, grad_features, grad_weight)
 
 

time: 378 us -> 293 us (0.78)
  waiting for transfers between devices: 166 us -> 76 us
    all_gather x0 -> x1, waiting for transfers between devices: none -> 64.9 us  [per_device(): lax.all_gather(weight_term, ('row', 'col'))]
    reduce_scatter x1, waiting for transfers between devices: 62.9 us -> 0.02 us  [per_device(): lax.psum_scatter(backward_totals, 'col', scatter_dimension=0, tiled=True)]
    psum x1 -> x0, waiting for transfers between devices: 50.3 us -> none  [per_device(): grad_weight = lax.psum(weight_term, ('row', 'col')) / math.sqrt(node_total)]
    all_gather x1, waiting for transfers between devices: 40.8 us -> 0.02 us  [per_device(): lax.all_gather(features, 'col', axis=0, tiled=True)]
    unnamed x10 -> x9, local copies, waits for them, and re-layouts: 15.9 us -> 19.4 us
  transfers between devices with their start and end apart: 4 -> 4, of which waited for: 4 -> 2; matrix products, arithmetic and copies ran while one was open for 22% -> 65% of each run, Pallas kernels for 0% -> 0%
where the time goes in v1:
time: 293 us; the launch traced here: 290 us
  other arithmetic  114 us (39%)
  waiting for transfers between devices  76 us (26%)
  matrix products  49 us (17%)
  local copies, waits for them, and re-layouts  30.2 us (10%)
  between operations  13.9 us (5%)
  blocking collectives  5.85 us (2%)
    all_gather x1, waiting for transfers between devices, per_device(): lax.all_gather(weight_term, ('row', 'col'))  64.9 us
    scatter-add x5, other arithmetic, forward_block(): jax.ops.segment_sum(products, segment_ids, num_segments=row_tiles + 1)  44.1 us
    scatter-add x5, other arithmetic, backward_block(): jax.ops.segment_sum(products, segment_ids, num_segments=col_tiles + 1)  44 us
    dot_general x5, matrix products, backward_block(): jnp.einsum('tab,taf->tbf', part_tiles, inputs, preferred_element_type=jnp...  21.9 us
    dot_general x5, matrix products, forward_block(): jnp.einsum('tab,tbf->taf', part_tiles, inputs, preferred_element_type=jnp...  21.2 us
    unnamed x9, local copies, waits for them, and re-layouts  19.4 us
    add x5, other arithmetic, backward_block(): return totals + summed[:col_tiles]  14.6 us
    reduce_scatter x1, waiting for transfers between devices, per_device(): lax.psum_scatter(forward_totals.reshape(row_tiles * tile_extent, output_w...  10.3 us
  transfers between devices with their start and end apart: 4, of which 2 were waited for; matrix products, arithmetic and copies ran while one was open for 65% of the time, Pallas kernels for 0%

profile of v1, /device:TPU:0, one launch (start us, length us, event | category | flops | bytes accessed | tf_op | source)
XLA Modules:
  0.0 289.8 jit_solution(16920349037195931348)
XLA Ops:
  9.4 14.4 %copy.12 = bf16[1,1,320,128,128]{3,4,2,1,0:T(8,128)(2,1)} copy(bf16[1,1,320,128,128]{4,3,2,1,0:T(8,128)(2,1)} %param.13) | data formatting | bytes 20971520 | tf_op args[2]
  23.8 5.9 %all_gather.13 = bf16[512,128]{1,0:T(8,128)(2,1)S(1)} all-gather(bf16[256,128]{1,0:T(8,128)(2,1)S(1)} %copy-done.2), channel_id=1, replica_groups=mesh['row'=2,'col'=16] {'row'}, dimensions={0}, use_global_device_ids=true | all-gather | bytes 196608 | tf_op jit(solution)/shard_map/all_gather | solution.py:59
  29.6 90.3 %while.29 = (s32[]{:T(128)}, f32[32,128,128]{2,1,0:T(8,128)}, s32[]{:T(128)}, s32[320]{0:T(512)S(1)}, bf16[320,128,128]{1,2,0:T(8,128)(2,1)}, /*index=5*/s32[320...) while((s32[]{:T(128)}, f32[32,128,128]{2,1,0:T(8,128)}, ...), condition=%wide.region_6.7_spmd.clone, body=%wide.region_4.6_spmd.clone.sunk | while | flops 270534272 | bytes 33626048 | solution.py:74
  30.4 1.0 gather_fusion.1
  31.3 4.4 %fusion.25 = f32[64,128,128]{2,1,0:T(8,128)} fusion(bf16[64,128,128]{2,1,0:T(8,128)(2,1)S(1)} %gather_fusion.1, bf16[320,128,128]{1,2,0:T(8,128)(2,1)} %get-tuple-element.508, s32[]{:T(128)S(6)} %select_n.64), kind=kOutput, calls=%fused_computation.12.clone.1 | convolution fusion | flops 268435456 | bytes 8388612 | tf_op jit(solution)/shard_map/while/body/eval_jaxpr/tab,taf->tbf/dot_general | solution.py:65
  36.0 8.8 %scatter_fusion.1 = f32[33,128,128]{2,1,0:T(8,128)S(1)} fusion(f32[33,128,128]{2,1,0:T(8,128)S(1)} %broadcast.112, s32[64]{0:T(128)S(1)} %get-tuple-element.442, f32[64,128,128]{2,1,0:T(8,128)} %fusion.25), kind=kCustom, calls=%fused_computation.3.clone.clone.1 | custom fusion | flops 1048576 | bytes 12583168 | tf_op jit(solution)/shard_map/while/body/eval_jaxpr/scatter-add | solution.py:70
  44.8 1.7 slice_add_fusion.5
  47.2 1.0 gather_fusion.1
  48.1 4.4 %fusion.25 = f32[64,128,128]{2,1,0:T(8,128)} fusion(bf16[64,128,128]{2,1,0:T(8,128)(2,1)S(1)} %gather_fusion.1, bf16[320,128,128]{1,2,0:T(8,128)(2,1)} %get-tuple-element.508, s32[]{:T(128)S(6)} %select_n.64), kind=kOutput, calls=%fused_computation.12.clone.1 | convolution fusion | flops 268435456 | bytes 8388612 | tf_op jit(solution)/shard_map/while/body/eval_jaxpr/tab,taf->tbf/dot_general | solution.py:65
  52.8 8.8 %scatter_fusion.1 = f32[33,128,128]{2,1,0:T(8,128)S(1)} fusion(f32[33,128,128]{2,1,0:T(8,128)S(1)} %broadcast.112, s32[64]{0:T(128)S(1)} %get-tuple-element.442, f32[64,128,128]{2,1,0:T(8,128)} %fusion.25), kind=kCustom, calls=%fused_computation.3.clone.clone.1 | custom fusion | flops 1048576 | bytes 12583168 | tf_op jit(solution)/shard_map/while/body/eval_jaxpr/scatter-add | solution.py:70
  61.6 3.2 %slice_add_fusion.5 = f32[32,128,128]{2,1,0:T(8,128)} fusion(f32[33,128,128]{2,1,0:T(8,128)S(1)} %scatter_fusion.1, f32[32,128,128]{2,1,0:T(8,128)} %get-tuple-element.493, pred[]{:T(512)S(6)} %compare.7), kind=kLoop, calls=%fused_computation.11.clone.1 | loop fusion | flops 1048576 | bytes 6291457 | tf_op jit(solution)/shard_map/while/body/eval_jaxpr/add | solution.py:71
  65.6 1.0 gather_fusion.1
  66.5 4.4 %fusion.25 = f32[64,128,128]{2,1,0:T(8,128)} fusion(bf16[64,128,128]{2,1,0:T(8,128)(2,1)S(1)} %gather_fusion.1, bf16[320,128,128]{1,2,0:T(8,128)(2,1)} %get-tuple-element.508, s32[]{:T(128)S(6)} %select_n.64), kind=kOutput, calls=%fused_computation.12.clone.1 | convolution fusion | flops 268435456 | bytes 8388612 | tf_op jit(solution)/shard_map/while/body/eval_jaxpr/tab,taf->tbf/dot_general | solution.py:65
  71.2 8.8 %scatter_fusion.1 = f32[33,128,128]{2,1,0:T(8,128)S(1)} fusion(f32[33,128,128]{2,1,0:T(8,128)S(1)} %broadcast.112, s32[64]{0:T(128)S(1)} %get-tuple-element.442, f32[64,128,128]{2,1,0:T(8,128)} %fusion.25), kind=kCustom, calls=%fused_computation.3.clone.clone.1 | custom fusion | flops 1048576 | bytes 12583168 | tf_op jit(solution)/shard_map/while/body/eval_jaxpr/scatter-add | solution.py:70
  80.0 3.2 %slice_add_fusion.5 = f32[32,128,128]{2,1,0:T(8,128)} fusion(f32[33,128,128]{2,1,0:T(8,128)S(1)} %scatter_fusion.1, f32[32,128,128]{2,1,0:T(8,128)} %get-tuple-element.493, pred[]{:T(512)S(6)} %compare.7), kind=kLoop, calls=%fused_computation.11.clone.1 | loop fusion | flops 1048576 | bytes 6291457 | tf_op jit(solution)/shard_map/while/body/eval_jaxpr/add | solution.py:71
  83.9 1.0 gather_fusion.1
  84.9 4.4 %fusion.25 = f32[64,128,128]{2,1,0:T(8,128)} fusion(bf16[64,128,128]{2,1,0:T(8,128)(2,1)S(1)} %gather_fusion.1, bf16[320,128,128]{1,2,0:T(8,128)(2,1)} %get-tuple-element.508, s32[]{:T(128)S(6)} %select_n.64), kind=kOutput, calls=%fused_computation.12.clone.1 | convolution fusion | flops 268435456 | bytes 8388612 | tf_op jit(solution)/shard_map/while/body/eval_jaxpr/tab,taf->tbf/dot_general | solution.py:65
  89.5 8.8 %scatter_fusion.1 = f32[33,128,128]{2,1,0:T(8,128)S(1)} fusion(f32[33,128,128]{2,1,0:T(8,128)S(1)} %broadcast.112, s32[64]{0:T(128)S(1)} %get-tuple-element.442, f32[64,128,128]{2,1,0:T(8,128)} %fusion.25), kind=kCustom, calls=%fused_computation.3.clone.clone.1 | custom fusion | flops 1048576 | bytes 12583168 | tf_op jit(solution)/shard_map/while/body/eval_jaxpr/scatter-add | solution.py:70
  98.3 3.2 %slice_add_fusion.5 = f32[32,128,128]{2,1,0:T(8,128)} fusion(f32[33,128,128]{2,1,0:T(8,128)S(1)} %scatter_fusion.1, f32[32,128,128]{2,1,0:T(8,128)} %get-tuple-element.493, pred[]{:T(512)S(6)} %compare.7), kind=kLoop, calls=%fused_computation.11.clone.1 | loop fusion | flops 1048576 | bytes 6291457 | tf_op jit(solution)/shard_map/while/body/eval_jaxpr/add | solution.py:71
  102.3 1.0 gather_fusion.1
  103.3 4.4 %fusion.25 = f32[64,128,128]{2,1,0:T(8,128)} fusion(bf16[64,128,128]{2,1,0:T(8,128)(2,1)S(1)} %gather_fusion.1, bf16[320,128,128]{1,2,0:T(8,128)(2,1)} %get-tuple-element.508, s32[]{:T(128)S(6)} %select_n.64), kind=kOutput, calls=%fused_computation.12.clone.1 | convolution fusion | flops 268435456 | bytes 8388612 | tf_op jit(solution)/shard_map/while/body/eval_jaxpr/tab,taf->tbf/dot_general | solution.py:65
  107.9 8.8 %scatter_fusion.1 = f32[33,128,128]{2,1,0:T(8,128)S(1)} fusion(f32[33,128,128]{2,1,0:T(8,128)S(1)} %broadcast.112, s32[64]{0:T(128)S(1)} %get-tuple-element.442, f32[64,128,128]{2,1,0:T(8,128)} %fusion.25), kind=kCustom, calls=%fused_computation.3.clone.clone.1 | custom fusion | flops 1048576 | bytes 12583168 | tf_op jit(solution)/shard_map/while/body/eval_jaxpr/scatter-add | solution.py:70
  116.7 3.2 %slice_add_fusion.5 = f32[32,128,128]{2,1,0:T(8,128)} fusion(f32[33,128,128]{2,1,0:T(8,128)S(1)} %scatter_fusion.1, f32[32,128,128]{2,1,0:T(8,128)} %get-tuple-element.493, pred[]{:T(512)S(6)} %compare.7), kind=kLoop, calls=%fused_computation.11.clone.1 | loop fusion | flops 1048576 | bytes 6291457 | tf_op jit(solution)/shard_map/while/body/eval_jaxpr/add | solution.py:71
  120.1 2.3 convolution_convert_fusion
  122.4 74.4 %while.28 = (s32[]{:T(128)}, f32[4,128,128]{2,1,0:T(8,128)S(1)}, s32[]{:T(128)}, s32[320]{0:T(512)S(1)}, bf16[320,128,128]{2,1,0:T(8,128)(2,1)}, /*index=5*/s32[...) while((s32[]{:T(128)}, f32[4,128,128]{2,1,0:T(8,128)S(1)}, ...), condition=%wide.region_2.3_spmd.clone, body=%wide.region_0.2_spmd.clone.sunk | while | flops 269616512 | bytes 26286016 | solution.py:47
  123.1 1.0 gather_fusion
  124.1 4.2 %fusion.22 = f32[64,128,128]{2,1,0:T(8,128)} fusion(bf16[64,128,128]{2,1,0:T(8,128)(2,1)S(1)} %gather_fusion, bf16[320,128,128]{2,1,0:T(8,128)(2,1)} %get-tuple-element.472, s32[]{:T(128)S(6)} %select_n.62), kind=kOutput, calls=%fused_computation.4.clone.1 | convolution fusion | flops 268435456 | bytes 8388612 | tf_op jit(solution)/shard_map/while/body/eval_jaxpr/tab,tbf->taf/dot_general | solution.py:40
  128.3 8.9 %scatter_fusion = f32[5,128,128]{2,1,0:T(8,128)S(1)} fusion(f32[5,128,128]{2,1,0:T(8,128)S(1)} %broadcast.105, s32[64]{0:T(128)S(1)} %get-tuple-element.433, f32[64,128,128]{2,1,0:T(8,128)} %fusion.22), kind=kCustom, calls=%fused_computation.2.clone.clone.1 | custom fusion | flops 1048576 | bytes 12583168 | tf_op jit(solution)/shard_map/while/body/eval_jaxpr/scatter-add | solution.py:44
  138.1 1.0 gather_fusion
  139.1 4.3 %fusion.22 = f32[64,128,128]{2,1,0:T(8,128)} fusion(bf16[64,128,128]{2,1,0:T(8,128)(2,1)S(1)} %gather_fusion, bf16[320,128,128]{2,1,0:T(8,128)(2,1)} %get-tuple-element.472, s32[]{:T(128)S(6)} %select_n.62), kind=kOutput, calls=%fused_computation.4.clone.1 | convolution fusion | flops 268435456 | bytes 8388612 | tf_op jit(solution)/shard_map/while/body/eval_jaxpr/tab,tbf->taf/dot_general | solution.py:40
  143.4 8.8 %scatter_fusion = f32[5,128,128]{2,1,0:T(8,128)S(1)} fusion(f32[5,128,128]{2,1,0:T(8,128)S(1)} %broadcast.105, s32[64]{0:T(128)S(1)} %get-tuple-element.433, f32[64,128,128]{2,1,0:T(8,128)} %fusion.22), kind=kCustom, calls=%fused_computation.2.clone.clone.1 | custom fusion | flops 1048576 | bytes 12583168 | tf_op jit(solution)/shard_map/while/body/eval_jaxpr/scatter-add | solution.py:44
  153.0 1.0 gather_fusion
  154.0 4.2 %fusion.22 = f32[64,128,128]{2,1,0:T(8,128)} fusion(bf16[64,128,128]{2,1,0:T(8,128)(2,1)S(1)} %gather_fusion, bf16[320,128,128]{2,1,0:T(8,128)(2,1)} %get-tuple-element.472, s32[]{:T(128)S(6)} %select_n.62), kind=kOutput, calls=%fused_computation.4.clone.1 | convolution fusion | flops 268435456 | bytes 8388612 | tf_op jit(solution)/shard_map/while/body/eval_jaxpr/tab,tbf->taf/dot_general | solution.py:40
  158.2 8.8 %scatter_fusion = f32[5,128,128]{2,1,0:T(8,128)S(1)} fusion(f32[5,128,128]{2,1,0:T(8,128)S(1)} %broadcast.105, s32[64]{0:T(128)S(1)} %get-tuple-element.433, f32[64,128,128]{2,1,0:T(8,128)} %fusion.22), kind=kCustom, calls=%fused_computation.2.clone.clone.1 | custom fusion | flops 1048576 | bytes 12583168 | tf_op jit(solution)/shard_map/while/body/eval_jaxpr/scatter-add | solution.py:44
  167.9 1.0 gather_fusion
  168.8 4.2 %fusion.22 = f32[64,128,128]{2,1,0:T(8,128)} fusion(bf16[64,128,128]{2,1,0:T(8,128)(2,1)S(1)} %gather_fusion, bf16[320,128,128]{2,1,0:T(8,128)(2,1)} %get-tuple-element.472, s32[]{:T(128)S(6)} %select_n.62), kind=kOutput, calls=%fused_computation.4.clone.1 | convolution fusion | flops 268435456 | bytes 8388612 | tf_op jit(solution)/shard_map/while/body/eval_jaxpr/tab,tbf->taf/dot_general | solution.py:40
  173.1 8.8 %scatter_fusion = f32[5,128,128]{2,1,0:T(8,128)S(1)} fusion(f32[5,128,128]{2,1,0:T(8,128)S(1)} %broadcast.105, s32[64]{0:T(128)S(1)} %get-tuple-element.433, f32[64,128,128]{2,1,0:T(8,128)} %fusion.22), kind=kCustom, calls=%fused_computation.2.clone.clone.1 | custom fusion | flops 1048576 | bytes 12583168 | tf_op jit(solution)/shard_map/while/body/eval_jaxpr/scatter-add | solution.py:44
  182.7 1.0 gather_fusion
  183.7 4.2 %fusion.22 = f32[64,128,128]{2,1,0:T(8,128)} fusion(bf16[64,128,128]{2,1,0:T(8,128)(2,1)S(1)} %gather_fusion, bf16[320,128,128]{2,1,0:T(8,128)(2,1)} %get-tuple-element.472, s32[]{:T(128)S(6)} %select_n.62), kind=kOutput, calls=%fused_computation.4.clone.1 | convolution fusion | flops 268435456 | bytes 8388612 | tf_op jit(solution)/shard_map/while/body/eval_jaxpr/tab,tbf->taf/dot_general | solution.py:40
  187.9 8.8 %scatter_fusion = f32[5,128,128]{2,1,0:T(8,128)S(1)} fusion(f32[5,128,128]{2,1,0:T(8,128)S(1)} %broadcast.105, s32[64]{0:T(128)S(1)} %get-tuple-element.433, f32[64,128,128]{2,1,0:T(8,128)} %fusion.22), kind=kCustom, calls=%fused_computation.2.clone.clone.1 | custom fusion | flops 1048576 | bytes 12583168 | tf_op jit(solution)/shard_map/while/body/eval_jaxpr/scatter-add | solution.py:44
  197.6 1.8 convolution_bitcast_fusion
  199.4 1.7 convolution_convert_fusion.1
  201.2 10.3 %reduce-scatter.3.cloned.1.call-done = f32[256,128]{1,0:T(8,128)} async-done(((f32[512,128]{1,0:T(8,128)}), f32[256,128]{1,0:T(8,128)}) %reduce-scatter.3.cloned.1.call-update) | async-done | bytes 131088 | tf_op jit(solution)/shard_map/reduce_scatter | solution.py:53
  211.5 1.5 convert_element_type.13
  213.1 64.9 %all-gather.6.cloned.1.call-done = f32[8192,128]{0,1:T(8,128)} async-done(((f32[256,128]{0,1:T(8,128)}), f32[8192,128]{0,1:T(8,128)}) %all-gather.6.cloned.1.call-update) | async-done | bytes 4194320 | tf_op jit(solution)/shard_map/all_gather | solution.py:86
  278.0 3.5 %copy.16 = f32[16,8,32,256]{3,2,1,0:T(8,128)S(1)} copy(f32[16,8,32,256]{3,1,2,0:T(8,128)} %bitcast.30) | data formatting | bytes 8388608
  281.5 1.0 bitcast_reduce_fusion
  282.5 0.8 copy.14
  (56 shorter events, 12.0 us)
Async XLA Ops:
  7.2 112.9 %copy-start = (bf16[256,128]{1,0:T(8,128)(2,1)S(1)}, bf16[256,128]{1,0:T(8,128)(2,1)}, u32[]{:S(2)}) copy-start(bf16[256,128]{1,0:T(8,128)(2,1)} %param.12) | copy-start | bytes 196612
  7.2 112.9 %all-gather.4.cloned.1.call-start = ((), (), s32[]{:S(2)}) async-start(), calls=%async_computation.2 | async-start | bytes 2228224 | tf_op jit(solution)/shard_map/all_gather | solution.py:24
  7.9 189.7 %reduce-scatter.5.cloned.1.call-start = ((), (), s32[]{:S(2)}) async-start(), calls=%async_computation.4 | async-start | bytes 2228224 | tf_op jit(solution)/shard_map/reduce_scatter | solution.py:77
  9.4 14.4 %copy-start.2 = (bf16[256,128]{1,0:T(8,128)(2,1)S(1)}, bf16[256,128]{1,0:T(8,128)(2,1)}, u32[]{:S(2)}) copy-start(bf16[256,128]{1,0:T(8,128)(2,1)} %param.17) | copy-start | bytes 196612
  120.0 91.5 %reduce-scatter.3.cloned.1.call-start = ((), (), s32[]{:S(2)}) async-start(), calls=%async_computation.3 | async-start | bytes 393216 | tf_op jit(solution)/shard_map/reduce_scatter | solution.py:53
  196.8 0.7 copy-start.1
  197.5 80.5 %all-gather.6.cloned.1.call-start = ((), (), s32[]{:S(2)}) async-start(), calls=%async_computation.5 | async-start | bytes 4325376 | tf_op jit(solution)/shard_map/all_gather | solution.py:86
Sparse Core Ops, SparseCore 0:
  10.1 44.1 all-gather.3
  120.1 63.6 reduce-scatter.4
  197.6 13.8 reduce-scatter.2
  214.8 63.1 all-gather.5
